TPU v7x, 32 devices: a whole 2x2x4 slice. The times are simulated.
32 devices in a mesh: wide: 8 (over z, y), fields: 4 (over x, core).
Axes of the slice: x: 2, y: 2, z: 4, core: 2. Of those that a mesh axis runs over, the one named last changes fastest.
Arguments:
- vectors: float32 [256, 16384], P('wide', 'fields'), may hold values from 0.03 to 82, as said below
- pivot_ids: int32 [8], replicated, may hold values from 0 to 255
Outputs:
- similarity: float32 [256, 4, 256], P('wide', None, 'fields')
Inputs may be any that keep to these rules, and one draw needn't show every extreme that they name: `vectors`: every entry is positive.
All inputs are finite; a program needn't handle non-finite values.
Results may differ from a plain program's by a relative error of at most 0.0003.
Values sent between devices are 32-bit elements; how exact they have to be, the bound alone decides.
A program may use at most 64 MiB of HBM per device.

v0:
```python
import jax
import jax.numpy as jnp
from jax import lax
from jax.sharding import PartitionSpec as P

STEPS = 4


def from_behind(value, axis, steps):
    count = lax.axis_size(axis)
    pairs = [(source, (source + steps) % count) for source in range(count)]
    return lax.ppermute(value, axis, pairs)


def triple_table(owned, pivots, minima, partner):
    with_pivot = jnp.sum(minima, axis=-1)
    pivot_side = jnp.sum(jnp.minimum(pivots[:, None, :], partner[None, :, :]), axis=-1)
    pair_side = jnp.sum(jnp.minimum(owned[:, None, :], partner[None, :, :]), axis=-1)
    triple = lax.map(
        lambda layer: jnp.sum(jnp.minimum(layer[:, None, :], partner[None, :, :]), axis=-1),
        jnp.transpose(minima, (1, 0, 2)),
    )
    return (
        with_pivot[:, :, None]
        + pivot_side[None, :, :]
        + pair_side[:, None, :]
        - jnp.transpose(triple, (1, 0, 2))
    )


def body(vectors, pivot_ids):
    row_count = vectors.shape[0]
    pivot_count = pivot_ids.shape[0]
    first_row = lax.axis_index("wide") * row_count
    chosen = (
        pivot_ids[:, None] == first_row + jnp.arange(row_count, dtype=jnp.int32)[None, :]
    ).astype(jnp.float32)
    pivot_part = jnp.dot(
        chosen, vectors, precision=lax.Precision.HIGHEST, preferred_element_type=jnp.float32
    )
    pivots = lax.psum(pivot_part, "wide")
    owned_total, pivot_total = lax.psum(
        (jnp.sum(vectors, axis=1), jnp.sum(pivots, axis=1)), "fields"
    )
    minima = jnp.minimum(vectors[:, None, :], pivots[None, :, :])
    partner, partner_total = (vectors, owned_total)
    numerators = []
    partner_totals = []
    for stride in range(1, STEPS + 1):
        partner, partner_total = from_behind((partner, partner_total), "wide", 1)
        partner_totals.append(partner_total)
        numerator = triple_table(vectors, pivots, minima, partner).reshape(
            row_count, pivot_count * row_count
        )
        numerators.append(numerator)
    stacked = jnp.stack(numerators, axis=1)
    shares = lax.psum_scatter(stacked, "fields", scatter_dimension=2, tiled=True)
    share_width = shares.shape[2]
    offset = lax.axis_index("fields") * share_width
    step_totals = jnp.stack(partner_totals, axis=0)
    denominator = (
        owned_total[:, None, None, None]
        + pivot_total[None, None, :, None]
        + step_totals[None, :, None, :]
    )
    denominator = denominator.reshape(row_count, STEPS, pivot_count * row_count)
    denominator = lax.dynamic_slice_in_dim(denominator, offset, share_width, 2)
    return 1.5 * shares / denominator


def solution(mesh):
    placed = (P("wide", "fields"), P())
    return jax.shard_map(
        body, mesh=mesh, in_specs=placed, out_specs=P("wide", None, "fields"), check_vma=False
    )
```

profile of v0, /device:TPU:0, one launch (start us, length us, event | category | flops | bytes accessed | tf_op | source)
XLA Modules:
  0.0 292.2 jit_solution(9529471152527923765)
XLA Ops:
  6.5 3.0 %collective-permute-start = (f32[32,4096]{1,0:T(8,128)}, f32[32,4096]{1,0:T(8,128)S(1)}, u32[]{:S(2)}, u32[]{:S(2)}) collective-permute-start(f32[32,4096]{1,0:T(8,128)} %param.10), channel_id=1, source_target_pairs={{0,4},{4,8},{8,12},{12,16},{16,20},{20,24},{24,28},{28,0},{1,5},{5... | collective-permute-start | bytes 1572872 | tf_op jit(solution)/shard_map/ppermute | solution.py:12
  9.5 15.2 %collective-permute-done = f32[32,4096]{1,0:T(8,128)S(1)} collective-permute-done((f32[32,4096]{1,0:T(8,128)}, f32[32,4096]{1,0:T(8,128)S(1)}, u32[]{:S(2)}, u32[]{:S(2)}) %collective-permute-start) | collective-permute-done | bytes 524320 | tf_op jit(solution)/shard_map/ppermute | solution.py:12
  24.7 15.8 %collective-permute-done.1 = f32[32,4096]{1,0:T(8,128)S(1)} collective-permute-done((f32[32,4096]{1,0:T(8,128)S(1)}, f32[32,4096]{1,0:T(8,128)S(1)}, u32[]{:S(2)}, u32[]{:S(2)}) %collective-permute-start.1) | collective-permute-done | bytes 524320 | tf_op jit(solution)/shard_map/ppermute | solution.py:12
  40.5 2.0 fusion
  42.6 13.3 %collective-permute-done.2 = f32[32,4096]{1,0:T(8,128)S(1)} collective-permute-done((f32[32,4096]{1,0:T(8,128)S(1)}, f32[32,4096]{1,0:T(8,128)S(1)}, u32[]{:S(2)}, u32[]{:S(2)}) %collective-permute-start.2) | collective-permute-done | bytes 524320 | tf_op jit(solution)/shard_map/ppermute | solution.py:12
  55.8 1.2 reduce_sum.156
  57.0 65.4 %all-reduce.3.cloned.1.call-done = f32[8,4096]{1,0:T(8,128)} async-done(((f32[8,4096]{1,0:T(8,128)}), f32[8,4096]{1,0:T(8,128)}) %all-reduce.3.cloned.1.call-update) | async-done | bytes 131088 | tf_op jit(solution)/shard_map/psum | solution.py:41
  123.4 5.7 %all-reduce = (f32[32]{0:T(128)S(1)}, f32[8]{0:T(128)S(1)}) all-reduce(f32[32]{0:T(128)S(1)} %reduce_sum.156, f32[8]{0:T(128)S(1)} %reduce_sum.157), channel_id=1, replica_groups=mesh['wide'=8,'fields'=4] {'fields'}, use_global_device_ids=true, to_apply=%region_24.25 | all-reduce | flops 40 | bytes 320 | tf_op jit(solution)/shard_map/psum | solution.py:42
  129.8 5.6 %collective-permute-done.4 = f32[32]{0:T(128)S(1)} collective-permute-done((f32[32]{0:T(128)S(1)}, f32[32]{0:T(128)S(1)}, u32[]{:S(2)}, u32[]{:S(2)}) %collective-permute-start.4) | collective-permute-done | bytes 160 | tf_op jit(solution)/shard_map/ppermute | solution.py:12
  135.4 1.5 minimum_reduce_fusion.12
  137.0 4.7 %collective-permute-done.5 = f32[32]{0:T(128)S(1)} collective-permute-done((f32[32]{0:T(128)S(1)}, f32[32]{0:T(128)S(1)}, u32[]{:S(2)}, u32[]{:S(2)}) %collective-permute-start.5) | collective-permute-done | bytes 160 | tf_op jit(solution)/shard_map/ppermute | solution.py:12
  141.9 6.1 %collective-permute-done.6 = f32[32]{0:T(128)S(1)} collective-permute-done((f32[32]{0:T(128)S(1)}, f32[32]{0:T(128)S(1)}, u32[]{:S(2)}, u32[]{:S(2)}) %collective-permute-start.6) | collective-permute-done | bytes 160 | tf_op jit(solution)/shard_map/ppermute | solution.py:12
  147.9 5.3 %minimum_reduce_fusion.11 = (f32[8,32]{1,0:T(8,128)S(1)}, f32[8,32]{1,0:T(8,128)S(1)}, f32[8,32]{1,0:T(8,128)S(1)}, f32[8,32]{1,0:T(8,128)S(1)}, f32[8,32,4096]{2,1,0:T(8,128)}) fusion(f32[32,4096]{1,0:T(8,128)S(1)} %collective-permute-done, f32[8,4096]{1,0:T(8,128)} %all-reduce.3.cloned.1.call-done, f32[32,4096]{1,0:T(8,128)S(1)} %collective-permute-done.1, ...), kind=kLoop, calls=%fused_computation.19 | loop fusion | flops 9436160 | bytes 6950912 | tf_op jit(solution)/shard_map/reduce_sum | solution.py:17
  153.2 25.6 %while.40 = (s32[]{:T(128)}, f32[8,32,32]{2,1,0:T(8,128)S(1)}, f32[8,32,4096]{2,1,0:T(8,128)}, f32[32,4096]{1,0:T(8,128)S(1)}, s32[]{:T(128)}) while((s32[]{:T(128)}, f32[8,32,32]{2,1,0:T(8,128)S(1)}, f32[8,32,4096]{2,1,0:T(8,128)}, f32[32,4096]{1,0:T(8,128)S(1)}, s32[]{:T(128)}) %tuple.67), condition=%wide.region_6.0_spmd, body=%wide.region_4.6_spmd.sunk | while | flops 8387586 | bytes 2134093 | solution.py:19
  153.4 1.1 dynamic-slice_bitcast_fusion.8
  154.5 2.1 minimum_reduce_fusion.17
  156.6 1.1 dynamic-slice_bitcast_fusion.8
  157.7 2.1 minimum_reduce_fusion.17
  159.8 1.1 dynamic-slice_bitcast_fusion.8
  160.8 2.1 minimum_reduce_fusion.17
  162.9 1.1 dynamic-slice_bitcast_fusion.8
  164.0 2.1 minimum_reduce_fusion.17
  166.1 1.1 dynamic-slice_bitcast_fusion.8
  167.2 2.1 minimum_reduce_fusion.17
  170.4 2.1 minimum_reduce_fusion.17
  172.5 1.1 dynamic-slice_bitcast_fusion.8
  173.6 2.1 minimum_reduce_fusion.17
  176.7 2.1 minimum_reduce_fusion.17
  178.9 25.4 %while.41 = (s32[]{:T(128)}, f32[8,32,32]{2,1,0:T(8,128)S(1)}, f32[8,32,4096]{2,1,0:T(8,128)}, f32[32,4096]{1,0:T(8,128)S(1)}, s32[]{:T(128)}) while((s32[]{:T(128)}, f32[8,32,32]{2,1,0:T(8,128)S(1)}, f32[8,32,4096]{2,1,0:T(8,128)}, f32[32,4096]{1,0:T(8,128)S(1)}, s32[]{:T(128)}) %tuple.83), condition=%wide.region_11.12_spmd, body=%wide.region_9.11_spmd.sunk | while | flops 8387586 | bytes 2134093 | solution.py:19
  179.9 2.1 minimum_reduce_fusion.18
  183.1 2.1 minimum_reduce_fusion.18
  185.2 1.1 dynamic-slice_bitcast_fusion.9
  186.3 2.1 minimum_reduce_fusion.18
  189.5 2.1 minimum_reduce_fusion.18
  192.7 2.1 minimum_reduce_fusion.18
  194.8 1.1 dynamic-slice_bitcast_fusion.9
  195.8 2.1 minimum_reduce_fusion.18
  199.0 2.1 minimum_reduce_fusion.18
  202.2 2.1 minimum_reduce_fusion.18
  204.3 25.4 %while.42 = (s32[]{:T(128)}, f32[8,32,32]{2,1,0:T(8,128)S(1)}, f32[8,32,4096]{2,1,0:T(8,128)}, f32[32,4096]{1,0:T(8,128)S(1)}, s32[]{:T(128)}) while((s32[]{:T(128)}, f32[8,32,32]{2,1,0:T(8,128)S(1)}, f32[8,32,4096]{2,1,0:T(8,128)}, f32[32,4096]{1,0:T(8,128)S(1)}, s32[]{:T(128)}) %tuple.84), condition=%wide.region_16.17_spmd, body=%wide.region_14.16_spmd.sunk | while | flops 8387586 | bytes 2134093 | solution.py:19
  205.4 2.1 minimum_reduce_fusion.19
  207.5 1.1 dynamic-slice_bitcast_fusion.10
  208.6 2.1 minimum_reduce_fusion.19
  211.8 2.1 minimum_reduce_fusion.19
  214.9 2.1 minimum_reduce_fusion.19
  217.0 1.1 dynamic-slice_bitcast_fusion.10
  218.1 2.1 minimum_reduce_fusion.19
  221.3 2.1 minimum_reduce_fusion.19
  224.5 2.1 minimum_reduce_fusion.19
  227.7 2.1 minimum_reduce_fusion.19
  229.8 25.5 %while.43 = (s32[]{:T(128)}, f32[8,32,32]{2,1,0:T(8,128)S(1)}, f32[8,32,4096]{2,1,0:T(8,128)}, f32[32,4096]{1,0:T(8,128)S(1)}, s32[]{:T(128)}) while((s32[]{:T(128)}, f32[8,32,32]{2,1,0:T(8,128)S(1)}, f32[8,32,4096]{2,1,0:T(8,128)}, f32[32,4096]{1,0:T(8,128)S(1)}, s32[]{:T(128)}) %tuple.85), condition=%wide.region_21.22_spmd, body=%wide.region_19.21_spmd.sunk | while | flops 8387586 | bytes 2134093 | solution.py:19
  229.8 1.1 dynamic-slice_bitcast_fusion.11
  230.9 2.1 minimum_reduce_fusion.20
  234.1 2.1 minimum_reduce_fusion.20
  237.3 2.1 minimum_reduce_fusion.20
  240.5 2.1 minimum_reduce_fusion.20
  242.6 1.1 dynamic-slice_bitcast_fusion.11
  243.6 2.1 minimum_reduce_fusion.20
  246.8 2.1 minimum_reduce_fusion.20
  250.0 2.1 minimum_reduce_fusion.20
  252.1 1.1 dynamic-slice_bitcast_fusion.11
  253.2 2.1 minimum_reduce_fusion.20
  255.3 4.9 %minimum_reduce_fusion.7 = (f32[32,32]{1,0:T(8,128)S(1)}, f32[32,32]{1,0:T(8,128)S(1)}, f32[32,32]{1,0:T(8,128)S(1)}, f32[32,32]{1,0:T(8,128)S(1)}) fusion(f32[32,4096]{1,0:T(8,128)S(1)} %get-tuple-element.311, f32[32,4096]{1,0:T(8,128)S(1)} %copy-done, f32[32,4096]{1,0:T(8,128)S(1)} %get-tuple-element.314, f32[32,4096]{1,0:T(8,128)S(1)} %get-tuple-element.317, ...), kind=kLoop, calls=%fused_computation.15 | loop fusion | flops 33550336 | bytes 2637824 | tf_op jit(solution)/shard_map/reduce_sum | solution.py:18
  262.6 21.2 %reduce-scatter.4.cloned.1.call-done = f32[64,128]{1,0:T(8,128)} async-done(((f32[256,128]{1,0:T(8,128)}), f32[64,128]{1,0:T(8,128)}) %reduce-scatter.4.cloned.1.call-update) | async-done | bytes 32784
  (97 shorter events, 26.8 us)
Async XLA Ops:
  6.5 115.9 %all-reduce.3.cloned.1.call-start = ((), (), s32[]{:S(2)}) async-start(), calls=%async_computation.1 | async-start | bytes 262144 | tf_op jit(solution)/shard_map/psum | solution.py:41
  6.5 18.2 %collective-permute-start = (f32[32,4096]{1,0:T(8,128)}, f32[32,4096]{1,0:T(8,128)S(1)}, u32[]{:S(2)}, u32[]{:S(2)}) collective-permute-start(f32[32,4096]{1,0:T(8,128)} %param.10), channel_id=1, source_target_pairs={{0,4},{4,8},{8,12},{12,16},{16,20},{20,24},{24,28},{28,0},{1,5},{5... | collective-permute-start | bytes 1572872 | tf_op jit(solution)/shard_map/ppermute | solution.py:12
  24.7 15.8 %collective-permute-start.1 = (f32[32,4096]{1,0:T(8,128)S(1)}, f32[32,4096]{1,0:T(8,128)S(1)}, u32[]{:S(2)}, u32[]{:S(2)}) collective-permute-start(f32[32,4096]{1,0:T(8,128)S(1)} %collective-permute-done), channel_id=1, source_target_pairs={{0,4},{4,8},{8,12},{12,16},{16,20},{20,24},{24,28},{28,0},{1,5},{5... | collective-permute-start | bytes 1572872 | tf_op jit(solution)/shard_map/ppermute | solution.py:12
  40.5 15.3 %collective-permute-start.2 = (f32[32,4096]{1,0:T(8,128)S(1)}, f32[32,4096]{1,0:T(8,128)S(1)}, u32[]{:S(2)}, u32[]{:S(2)}) collective-permute-start(f32[32,4096]{1,0:T(8,128)S(1)} %collective-permute-done.1), channel_id=1, source_target_pairs={{0,4},{4,8},{8,12},{12,16},{16,20},{20,24},{24,28},{28,0},{1,5},{5... | collective-permute-start | bytes 1572872 | tf_op jit(solution)/shard_map/ppermute | solution.py:12
  42.5 241.2 %reduce-scatter.4.cloned.1.call-start = ((), (), s32[]{:S(2)}) async-start(), calls=%async_computation.2 | async-start | bytes 163840
  55.8 92.1 %collective-permute-start.3 = (f32[32,4096]{1,0:T(8,128)S(1)}, f32[32,4096]{1,0:T(8,128)S(1)}, u32[]{:S(2)}, u32[]{:S(2)}) collective-permute-start(f32[32,4096]{1,0:T(8,128)S(1)} %collective-permute-done.2), channel_id=1, source_target_pairs={{0,4},{4,8},{8,12},{12,16},{16,20},{20,24},{24,28},{28,0},{1,5},{5... | collective-permute-start | bytes 1572872 | tf_op jit(solution)/shard_map/ppermute | solution.py:12
  129.1 6.3 %collective-permute-start.4 = (f32[32]{0:T(128)S(1)}, f32[32]{0:T(128)S(1)}, u32[]{:S(2)}, u32[]{:S(2)}) collective-permute-start(f32[32]{0:T(128)S(1)} %get-tuple-element.137), channel_id=1, source_target_pairs={{0,4},{4,8},{8,12},{12,16},{16,20},{20,24},{24,28},{28,0},{1,5},{5... | collective-permute-start | bytes 392 | tf_op jit(solution)/shard_map/ppermute | solution.py:12
  135.4 6.3 %collective-permute-start.5 = (f32[32]{0:T(128)S(1)}, f32[32]{0:T(128)S(1)}, u32[]{:S(2)}, u32[]{:S(2)}) collective-permute-start(f32[32]{0:T(128)S(1)} %collective-permute-done.4), channel_id=1, source_target_pairs={{0,4},{4,8},{8,12},{12,16},{16,20},{20,24},{24,28},{28,0},{1,5},{5... | collective-permute-start | bytes 392 | tf_op jit(solution)/shard_map/ppermute | solution.py:12
  141.7 6.3 %collective-permute-start.6 = (f32[32]{0:T(128)S(1)}, f32[32]{0:T(128)S(1)}, u32[]{:S(2)}, u32[]{:S(2)}) collective-permute-start(f32[32]{0:T(128)S(1)} %collective-permute-done.5), channel_id=1, source_target_pairs={{0,4},{4,8},{8,12},{12,16},{16,20},{20,24},{24,28},{28,0},{1,5},{5... | collective-permute-start | bytes 392 | tf_op jit(solution)/shard_map/ppermute | solution.py:12
  147.9 114.4 %collective-permute-start.7 = (f32[32]{0:T(128)S(1)}, f32[32]{0:T(128)S(1)}, u32[]{:S(2)}, u32[]{:S(2)}) collective-permute-start(f32[32]{0:T(128)S(1)} %collective-permute-done.6), channel_id=1, source_target_pairs={{0,4},{4,8},{8,12},{12,16},{16,20},{20,24},{24,28},{28,0},{1,5},{5... | collective-permute-start | bytes 392 | tf_op jit(solution)/shard_map/ppermute | solution.py:12
  229.8 25.5 %copy-start = (f32[32,4096]{1,0:T(8,128)S(1)}, f32[32,4096]{1,0:T(8,128)}, u32[]{:S(2)}) copy-start(f32[32,4096]{1,0:T(8,128)} %param.10) | copy-start | bytes 1572868
Sparse Core Ops, SparseCore 0:
  42.6 79.7 all-reduce.2
  262.4 21.2 reduce-scatter.3
where the time goes:
time: 294 us; the launch traced here: 292 us
  waiting for transfers between devices  147 us (50%)
  other arithmetic  80.9 us (28%)
  local copies, waits for them, and re-layouts  38.8 us (13%)
  between operations  13.6 us (5%)
  blocking collectives  5.66 us (2%)
  starting transfers between devices  3.69 us (1%)
    reduce_sum x32, other arithmetic, triple_table(): jnp.sum(jnp.minimum(layer[:, None, :], partner[None, :, :]), axis=-1)  66.7 us
    psum x1, waiting for transfers between devices, body(): pivots = lax.psum(pivot_part, 'wide')  65.4 us
    ppermute x8, waiting for transfers between devices, from_behind(): return lax.ppermute(value, axis, pairs)  60.6 us
    min x32, local copies, waits for them, and re-layouts, triple_table(): jnp.minimum(layer[:, None, :], partner[None, :, :])  34.6 us
    unnamed x3, waiting for transfers between devices  21.2 us
  transfers between devices with their start and end apart: 10, of which 8 were waited for; matrix products, arithmetic and copies ran while one was open for 41% of the time, Pallas kernels for 0%

commit v1 on v0

--- a/solution.py
+++ b/solution.py
@@ -38,7 +38,7 @@
     pivot_part = jnp.dot(
         chosen, vectors, precision=lax.Precision.HIGHEST, preferred_element_type=jnp.float32
     )
-    pivots = lax.psum(pivot_part, "wide")
+    pivots = jnp.sum(lax.all_gather(pivot_part, "wide"), axis=0)
     owned_total, pivot_total = lax.psum(
         (jnp.sum(vectors, axis=1), jnp.sum(pivots, axis=1)), "fields"
     )

time: 294 us -> 245 us (0.83)
  waiting for transfers between devices: 147 us -> 84.5 us
  starting transfers between devices: 3.69 us -> 16.7 us
    psum x1 -> x0, waiting for transfers between devices: 65.4 us -> none  [body(): pivots = lax.psum(pivot_part, 'wide')]
    ppermute x8, starting transfers between devices: 3.65 us -> 16.7 us  [from_behind(): return lax.ppermute(value, axis, pairs)]
  transfers between devices with their start and end apart: 10 -> 10, of which waited for: 8 -> 7; matrix products, arithmetic and copies ran while one was open for 41% -> 49% of each run, Pallas kernels for 0% -> 0%
where the time goes in v1:
time: 245 us; the launch traced here: 243 us
  waiting for transfers between devices  84.5 us (34%)
  other arithmetic  81.4 us (33%)
  local copies, waits for them, and re-layouts  38.8 us (16%)
  starting transfers between devices  16.7 us (7%)
  between operations  13.6 us (6%)
  blocking collectives  5.96 us (2%)
    reduce_sum x32, other arithmetic, triple_table(): jnp.sum(jnp.minimum(layer[:, None, :], partner[None, :, :]), axis=-1)  66.7 us
    ppermute x8, waiting for transfers between devices, from_behind(): return lax.ppermute(value, axis, pairs)  61.6 us
    min x32, local copies, waits for them, and re-layouts, triple_table(): jnp.minimum(layer[:, None, :], partner[None, :, :])  34.6 us
    unnamed x3, waiting for transfers between devices  21.2 us
    ppermute x8, starting transfers between devices, from_behind(): return lax.ppermute(value, axis, pairs)  16.7 us
    psum x1, blocking collectives, body(): lax.psum((jnp.sum(vectors, axis=1), jnp.sum(pivots, axis=1)), 'fields')  5.96 us
    reduce_sum x1, other arithmetic, triple_table(): jnp.sum(jnp.minimum(owned[:, None, :], partner[None, :, :]), axis=-1)  4.93 us
  transfers between devices with their start and end apart: 10, of which 7 were waited for; matrix products, arithmetic and copies ran while one was open for 49% of the time, Pallas kernels for 0%

profile of v1, /device:TPU:0, one launch (start us, length us, event | category | flops | bytes accessed | tf_op | source)
XLA Modules:
  0.0 243.4 jit_solution(17380839896470327873)
XLA Ops:
  6.5 2.1 fusion
  8.7 3.0 %collective-permute-start = (f32[32,4096]{1,0:T(8,128)}, f32[32,4096]{1,0:T(8,128)S(1)}, u32[]{:S(2)}, u32[]{:S(2)}) collective-permute-start(f32[32,4096]{1,0:T(8,128)} %param.10), channel_id=1, source_target_pairs={{0,4},{4,8},{8,12},{12,16},{16,20},{20,24},{24,28},{28,0},{1,5},{5... | collective-permute-start | bytes 1572872 | tf_op jit(solution)/shard_map/ppermute | solution.py:12
  11.7 16.8 %collective-permute-done = f32[32,4096]{1,0:T(8,128)S(1)} collective-permute-done((f32[32,4096]{1,0:T(8,128)}, f32[32,4096]{1,0:T(8,128)S(1)}, u32[]{:S(2)}, u32[]{:S(2)}) %collective-permute-start) | collective-permute-done | bytes 524320 | tf_op jit(solution)/shard_map/ppermute | solution.py:12
  28.5 15.4 %collective-permute-done.1 = f32[32,4096]{1,0:T(8,128)S(1)} collective-permute-done((f32[32,4096]{1,0:T(8,128)S(1)}, f32[32,4096]{1,0:T(8,128)S(1)}, u32[]{:S(2)}, u32[]{:S(2)}) %collective-permute-start.1) | collective-permute-done | bytes 524320 | tf_op jit(solution)/shard_map/ppermute | solution.py:12
  43.9 1.2 reduce_sum.166
  45.1 20.7 %collective-permute-done.2 = f32[32,4096]{1,0:T(8,128)S(1)} collective-permute-done((f32[32,4096]{1,0:T(8,128)S(1)}, f32[32,4096]{1,0:T(8,128)S(1)}, u32[]{:S(2)}, u32[]{:S(2)}) %collective-permute-start.2) | collective-permute-done | bytes 524320 | tf_op jit(solution)/shard_map/ppermute | solution.py:12
  65.8 1.6 all-gather.3.cloned.1.call-done
  67.5 1.4 reduce.1
  68.9 6.0 %all-reduce = (f32[32]{0:T(128)S(1)}, f32[8]{0:T(128)S(1)}) all-reduce(f32[32]{0:T(128)S(1)} %reduce_sum.166, f32[8]{0:T(128)S(1)} %reduce_sum.167), channel_id=1, replica_groups=mesh['wide'=8,'fields'=4] {'fields'}, use_global_device_ids=true, to_apply=%region_24.25 | all-reduce | flops 40 | bytes 320 | tf_op jit(solution)/shard_map/psum | solution.py:42
  74.9 11.4 %collective-permute-start.4 = (f32[32]{0:T(128)S(1)}, f32[32]{0:T(128)S(1)}, u32[]{:S(2)}, u32[]{:S(2)}) collective-permute-start(f32[32]{0:T(128)S(1)} %get-tuple-element.137), channel_id=1, source_target_pairs={{0,4},{4,8},{8,12},{12,16},{16,20},{20,24},{24,28},{28,0},{1,5},{5... | collective-permute-start | bytes 392 | tf_op jit(solution)/shard_map/ppermute | solution.py:12
  86.4 1.3 bitcast_reduce_fusion
  87.7 2.2 collective-permute-start.5
  89.9 1.4 minimum_reduce_fusion.12
  91.4 2.6 %collective-permute-done.5 = f32[32]{0:T(128)S(1)} collective-permute-done((f32[32]{0:T(128)S(1)}, f32[32]{0:T(128)S(1)}, u32[]{:S(2)}, u32[]{:S(2)}) %collective-permute-start.5) | collective-permute-done | bytes 160 | tf_op jit(solution)/shard_map/ppermute | solution.py:12
  94.2 6.1 %collective-permute-done.6 = f32[32]{0:T(128)S(1)} collective-permute-done((f32[32]{0:T(128)S(1)}, f32[32]{0:T(128)S(1)}, u32[]{:S(2)}, u32[]{:S(2)}) %collective-permute-start.6) | collective-permute-done | bytes 160 | tf_op jit(solution)/shard_map/ppermute | solution.py:12
  100.3 4.1 %minimum_reduce_fusion.11 = (f32[8,32]{1,0:T(8,128)S(1)}, f32[8,32]{1,0:T(8,128)S(1)}, f32[8,32]{1,0:T(8,128)S(1)}, f32[8,32]{1,0:T(8,128)S(1)}, f32[8,32,4096]{2,1,0:T(8,128)}) fusion(f32[32,4096]{1,0:T(8,128)S(1)} %collective-permute-done, f32[8,4096]{1,0:T(8,128)S(1)} %bitcast_reduce_fusion, f32[32,4096]{1,0:T(8,128)S(1)} %collective-permute-done.1, ...), kind=kLoop, calls=%fused_computation.19 | loop fusion | flops 9436160 | bytes 6950912 | tf_op jit(solution)/shard_map/reduce_sum | solution.py:17
  104.5 25.6 %while.43 = (s32[]{:T(128)}, f32[8,32,32]{2,1,0:T(8,128)S(1)}, f32[8,32,4096]{2,1,0:T(8,128)}, f32[32,4096]{1,0:T(8,128)S(1)}, s32[]{:T(128)}) while((s32[]{:T(128)}, f32[8,32,32]{2,1,0:T(8,128)S(1)}, f32[8,32,4096]{2,1,0:T(8,128)}, f32[32,4096]{1,0:T(8,128)S(1)}, s32[]{:T(128)}) %tuple.76), condition=%wide.region_21.22_spmd, body=%wide.region_19.21_spmd.sunk | while | flops 8387586 | bytes 2134093 | solution.py:19
  104.6 1.1 dynamic-slice_bitcast_fusion.11
  105.7 2.1 minimum_reduce_fusion.20
  108.9 2.1 minimum_reduce_fusion.20
  111.0 1.1 dynamic-slice_bitcast_fusion.11
  112.1 2.1 minimum_reduce_fusion.20
  114.2 1.1 dynamic-slice_bitcast_fusion.11
  115.3 2.1 minimum_reduce_fusion.20
  117.4 1.1 dynamic-slice_bitcast_fusion.11
  118.4 2.1 minimum_reduce_fusion.20
  120.5 1.1 dynamic-slice_bitcast_fusion.11
  121.6 2.1 minimum_reduce_fusion.20
  123.7 1.1 dynamic-slice_bitcast_fusion.11
  124.8 2.1 minimum_reduce_fusion.20
  126.9 1.1 dynamic-slice_bitcast_fusion.11
  128.0 2.1 minimum_reduce_fusion.20
  130.1 25.4 %while.42 = (s32[]{:T(128)}, f32[8,32,32]{2,1,0:T(8,128)S(1)}, f32[8,32,4096]{2,1,0:T(8,128)}, f32[32,4096]{1,0:T(8,128)S(1)}, s32[]{:T(128)}) while((s32[]{:T(128)}, f32[8,32,32]{2,1,0:T(8,128)S(1)}, f32[8,32,4096]{2,1,0:T(8,128)}, f32[32,4096]{1,0:T(8,128)S(1)}, s32[]{:T(128)}) %tuple.83), condition=%wide.region_16.17_spmd, body=%wide.region_14.16_spmd.sunk | while | flops 8387586 | bytes 2134093 | solution.py:19
  131.2 2.1 minimum_reduce_fusion.19
  134.4 2.1 minimum_reduce_fusion.19
  137.5 2.1 minimum_reduce_fusion.19
  140.7 2.1 minimum_reduce_fusion.19
  143.9 2.1 minimum_reduce_fusion.19
  146.0 1.1 dynamic-slice_bitcast_fusion.10
  147.1 2.1 minimum_reduce_fusion.19
  149.2 1.1 dynamic-slice_bitcast_fusion.10
  150.3 2.1 minimum_reduce_fusion.19
  152.4 1.1 dynamic-slice_bitcast_fusion.10
  153.4 2.1 minimum_reduce_fusion.19
  155.5 25.4 %while.41 = (s32[]{:T(128)}, f32[8,32,32]{2,1,0:T(8,128)S(1)}, f32[8,32,4096]{2,1,0:T(8,128)}, f32[32,4096]{1,0:T(8,128)S(1)}, s32[]{:T(128)}) while((s32[]{:T(128)}, f32[8,32,32]{2,1,0:T(8,128)S(1)}, f32[8,32,4096]{2,1,0:T(8,128)}, f32[32,4096]{1,0:T(8,128)S(1)}, s32[]{:T(128)}) %tuple.84), condition=%wide.region_11.12_spmd, body=%wide.region_9.11_spmd.sunk | while | flops 8387586 | bytes 2134093 | solution.py:19
  156.6 2.1 minimum_reduce_fusion.18
  159.8 2.1 minimum_reduce_fusion.18
  163.0 2.1 minimum_reduce_fusion.18
  166.2 2.1 minimum_reduce_fusion.18
  169.4 2.1 minimum_reduce_fusion.18
  172.5 2.1 minimum_reduce_fusion.18
  175.7 2.1 minimum_reduce_fusion.18
  178.9 2.1 minimum_reduce_fusion.18
  181.0 25.4 %while.40 = (s32[]{:T(128)}, f32[8,32,32]{2,1,0:T(8,128)S(1)}, f32[8,32,4096]{2,1,0:T(8,128)}, f32[32,4096]{1,0:T(8,128)S(1)}, s32[]{:T(128)}) while((s32[]{:T(128)}, f32[8,32,32]{2,1,0:T(8,128)S(1)}, f32[8,32,4096]{2,1,0:T(8,128)}, f32[32,4096]{1,0:T(8,128)S(1)}, s32[]{:T(128)}) %tuple.85), condition=%wide.region_6.0_spmd, body=%wide.region_4.6_spmd.sunk | while | flops 8387586 | bytes 2134093 | solution.py:19
  182.1 2.1 minimum_reduce_fusion.17
  185.3 2.1 minimum_reduce_fusion.17
  188.5 2.1 minimum_reduce_fusion.17
  191.6 2.1 minimum_reduce_fusion.17
  194.8 2.1 minimum_reduce_fusion.17
  198.0 2.1 minimum_reduce_fusion.17
  201.2 2.1 minimum_reduce_fusion.17
  204.3 2.1 minimum_reduce_fusion.17
  206.4 4.9 %minimum_reduce_fusion.7 = (f32[32,32]{1,0:T(8,128)S(1)}, f32[32,32]{1,0:T(8,128)S(1)}, f32[32,32]{1,0:T(8,128)S(1)}, f32[32,32]{1,0:T(8,128)S(1)}) fusion(f32[32,4096]{1,0:T(8,128)S(1)} %get-tuple-element.311, f32[32,4096]{1,0:T(8,128)S(1)} %copy-done, f32[32,4096]{1,0:T(8,128)S(1)} %get-tuple-element.314, f32[32,4096]{1,0:T(8,128)S(1)} %get-tuple-element.317, ...), kind=kLoop, calls=%fused_computation.15 | loop fusion | flops 33550336 | bytes 2637824 | tf_op jit(solution)/shard_map/reduce_sum | solution.py:18
  213.7 21.2 %reduce-scatter.4.cloned.1.call-done = f32[64,128]{1,0:T(8,128)} async-done(((f32[256,128]{1,0:T(8,128)}), f32[64,128]{1,0:T(8,128)}) %reduce-scatter.4.cloned.1.call-update) | async-done | bytes 32784
  (100 shorter events, 28.4 us)
Async XLA Ops:
  6.5 93.8 %copy-start = (f32[32,4096]{1,0:T(8,128)S(1)}, f32[32,4096]{1,0:T(8,128)}, u32[]{:S(2)}) copy-start(f32[32,4096]{1,0:T(8,128)} %param.10) | copy-start | bytes 1572868
  6.5 60.9 %all-gather.3.cloned.1.call-start = ((), (), s32[]{:S(2)}) async-start(), calls=%async_computation.1 | async-start | bytes 1179648 | tf_op jit(solution)/shard_map/all_gather | solution.py:41
  8.6 226.3 %reduce-scatter.4.cloned.1.call-start = ((), (), s32[]{:S(2)}) async-start(), calls=%async_computation.2 | async-start | bytes 163840
  8.7 19.8 %collective-permute-start = (f32[32,4096]{1,0:T(8,128)}, f32[32,4096]{1,0:T(8,128)S(1)}, u32[]{:S(2)}, u32[]{:S(2)}) collective-permute-start(f32[32,4096]{1,0:T(8,128)} %param.10), channel_id=1, source_target_pairs={{0,4},{4,8},{8,12},{12,16},{16,20},{20,24},{24,28},{28,0},{1,5},{5... | collective-permute-start | bytes 1572872 | tf_op jit(solution)/shard_map/ppermute | solution.py:12
  28.5 15.4 %collective-permute-start.1 = (f32[32,4096]{1,0:T(8,128)S(1)}, f32[32,4096]{1,0:T(8,128)S(1)}, u32[]{:S(2)}, u32[]{:S(2)}) collective-permute-start(f32[32,4096]{1,0:T(8,128)S(1)} %collective-permute-done), channel_id=1, source_target_pairs={{0,4},{4,8},{8,12},{12,16},{16,20},{20,24},{24,28},{28,0},{1,5},{5... | collective-permute-start | bytes 1572872 | tf_op jit(solution)/shard_map/ppermute | solution.py:12
  43.9 21.9 %collective-permute-start.2 = (f32[32,4096]{1,0:T(8,128)S(1)}, f32[32,4096]{1,0:T(8,128)S(1)}, u32[]{:S(2)}, u32[]{:S(2)}) collective-permute-start(f32[32,4096]{1,0:T(8,128)S(1)} %collective-permute-done.1), channel_id=1, source_target_pairs={{0,4},{4,8},{8,12},{12,16},{16,20},{20,24},{24,28},{28,0},{1,5},{5... | collective-permute-start | bytes 1572872 | tf_op jit(solution)/shard_map/ppermute | solution.py:12
  65.8 34.5 %collective-permute-start.3 = (f32[32,4096]{1,0:T(8,128)S(1)}, f32[32,4096]{1,0:T(8,128)S(1)}, u32[]{:S(2)}, u32[]{:S(2)}) collective-permute-start(f32[32,4096]{1,0:T(8,128)S(1)} %collective-permute-done.2), channel_id=1, source_target_pairs={{0,4},{4,8},{8,12},{12,16},{16,20},{20,24},{24,28},{28,0},{1,5},{5... | collective-permute-start | bytes 1572872 | tf_op jit(solution)/shard_map/ppermute | solution.py:12
  74.9 12.8 %collective-permute-start.4 = (f32[32]{0:T(128)S(1)}, f32[32]{0:T(128)S(1)}, u32[]{:S(2)}, u32[]{:S(2)}) collective-permute-start(f32[32]{0:T(128)S(1)} %get-tuple-element.137), channel_id=1, source_target_pairs={{0,4},{4,8},{8,12},{12,16},{16,20},{20,24},{24,28},{28,0},{1,5},{5... | collective-permute-start | bytes 392 | tf_op jit(solution)/shard_map/ppermute | solution.py:12
  87.7 6.3 %collective-permute-start.5 = (f32[32]{0:T(128)S(1)}, f32[32]{0:T(128)S(1)}, u32[]{:S(2)}, u32[]{:S(2)}) collective-permute-start(f32[32]{0:T(128)S(1)} %collective-permute-done.4), channel_id=1, source_target_pairs={{0,4},{4,8},{8,12},{12,16},{16,20},{20,24},{24,28},{28,0},{1,5},{5... | collective-permute-start | bytes 392 | tf_op jit(solution)/shard_map/ppermute | solution.py:12
  94.0 6.3 %collective-permute-start.6 = (f32[32]{0:T(128)S(1)}, f32[32]{0:T(128)S(1)}, u32[]{:S(2)}, u32[]{:S(2)}) collective-permute-start(f32[32]{0:T(128)S(1)} %collective-permute-done.5), channel_id=1, source_target_pairs={{0,4},{4,8},{8,12},{12,16},{16,20},{20,24},{24,28},{28,0},{1,5},{5... | collective-permute-start | bytes 392 | tf_op jit(solution)/shard_map/ppermute | solution.py:12
  100.3 113.2 %collective-permute-start.7 = (f32[32]{0:T(128)S(1)}, f32[32]{0:T(128)S(1)}, u32[]{:S(2)}, u32[]{:S(2)}) collective-permute-start(f32[32]{0:T(128)S(1)} %collective-permute-done.6), channel_id=1, source_target_pairs={{0,4},{4,8},{8,12},{12,16},{16,20},{20,24},{24,28},{28,0},{1,5},{5... | collective-permute-start | bytes 392 | tf_op jit(solution)/shard_map/ppermute | solution.py:12
Sparse Core Ops, SparseCore 0:
  9.5 57.9 all-gather.2
  213.6 21.2 reduce-scatter.3
